TPU v7x, 128 devices: a whole 4x4x4 slice. The times are simulated.
128 devices in a mesh: row: 32 (over z, y, core), col: 4 (over x).
Axes of the slice: x: 4, y: 4, z: 4, core: 2. Of those that a mesh axis runs over, the one named last changes fastest.
Arguments:
- positions: bfloat16 [8192, 64], P('row'), as said below
- log_weights: float32 [8192], P('row'), may hold values from 95 to 145
- cotangent: bfloat16 [8192, 64], P('row'), may hold values from -6 to 6
Outputs:
- grad_positions: float32 [8192, 64], P(('row', 'col'))
- grad_log_weights: float32 [8192], P('row')
Inputs may be any that keep to these rules, and one draw needn't show every extreme that they name: `positions`: particle states are finite real vectors.
All inputs are finite; a program needn't handle non-finite values.
Results may differ from a plain program's by a relative error of at most 0.008.
Values may be sent and summed in bfloat16 or wider, within the bound.
No kernel may reach another device: no remote copies, remote signals or barrier semaphores. Data moves between devices by JAX's collectives and lax.ppermute only.
A program may use at most 64 MiB of HBM per device.

v0:
```python
import math
import jax
import jax.numpy as jnp
from jax import lax
from jax.sharding import PartitionSpec as P

ITERS = 5


def row_lse(logits):
    highest = lax.pmax(jnp.max(logits, axis=1), "col")
    total_mass = lax.psum(jnp.sum(jnp.exp(logits - highest[:, None]), axis=1), "col")
    return highest + jnp.log(total_mass)


def column_lse(logits):
    highest = lax.pmax(jnp.max(logits, axis=0), "row")
    total_mass = lax.psum(jnp.sum(jnp.exp(logits - highest[None, :]), axis=0), "row")
    return highest + jnp.log(total_mass)


def local(positions, log_weights, cotangent):
    row_count = positions.shape[0]
    feature_dim = positions.shape[1]
    col_count = lax.axis_size("col")
    piece_len = row_count // col_count
    offset = lax.axis_index("col") * piece_len
    own_pos = lax.dynamic_slice_in_dim(positions, offset, piece_len, 0)
    own_cot = lax.dynamic_slice_in_dim(cotangent, offset, piece_len, 0)
    col_pos, col_cot = (
        lax.all_gather(own_pos, "row", axis=0, tiled=True),
        lax.all_gather(own_cot, "row", axis=0, tiled=True),
    )
    particle_total = col_pos.shape[0] * col_count
    log_count = math.log(particle_total)
    cost_scale = 4.0 / feature_dim
    row_f32 = positions.astype(jnp.float32)
    col_f32 = col_pos.astype(jnp.float32)
    row_sq = jnp.sum(row_f32 * row_f32, axis=1)
    col_sq = jnp.sum(col_f32 * col_f32, axis=1)

    def distances():
        cross = lax.dot_general(
            positions, col_pos, (((1,), (1,)), ((), ())), preferred_element_type=jnp.float32
        )
        return cost_scale * (row_sq[:, None] + col_sq[None, :] - 2.0 * cross)

    col_pot = jnp.zeros((col_pos.shape[0],), jnp.float32)
    rows_saved = []
    cols_saved = [col_pot]
    for section in range(ITERS):
        cost_tile = distances()
        row_pot = log_count - row_lse(col_pot[None, :] - cost_tile)
        col_pot = -column_lse(row_pot[:, None] + log_weights[:, None] - cost_tile)
        rows_saved.append(row_pot)
        cols_saved.append(col_pot)
    cost_tile = distances()
    transport = jnp.exp(
        rows_saved[-1][:, None] + cols_saved[-1][None, :] + log_weights[:, None] - cost_tile
    )
    paired = lax.dot_general(
        positions, col_cot, (((1,), (1,)), ((), ())), preferred_element_type=jnp.float32
    )
    weighted = transport * paired
    gradient_tile = -weighted
    col_grad = lax.psum(jnp.sum(weighted, axis=0), "row")
    surplus = jnp.sum(weighted, axis=1)
    grad_log_weights = jnp.zeros((row_count,), jnp.float32)
    for section in reversed(range(ITERS)):
        if section < ITERS - 1:
            cost_tile = distances()
        upper = rows_saved[section]
        column_soft = jnp.exp(
            upper[:, None] + log_weights[:, None] - cost_tile + cols_saved[section + 1][None, :]
        )
        row_grad = lax.psum(surplus - jnp.sum(column_soft * col_grad[None, :], axis=1), "col")
        surplus = jnp.zeros((row_count,), jnp.float32)
        back_tile = jnp.exp(cols_saved[section][None, :] - cost_tile + upper[:, None] - log_count)
        gradient_tile = (
            gradient_tile + column_soft * col_grad[None, :] + back_tile * row_grad[:, None]
        )
        grad_log_weights = grad_log_weights + row_grad
        if section > 0:
            col_grad = -lax.psum(jnp.sum(back_tile * row_grad[:, None], axis=0), "row")
    row_mass = jnp.sum(gradient_tile, axis=1)
    col_mass = jnp.sum(gradient_tile, axis=0)
    narrow = gradient_tile.astype(jnp.bfloat16)
    direct = jnp.dot(transport.astype(jnp.bfloat16), col_cot, preferred_element_type=jnp.float32)
    pulled = jnp.dot(narrow, col_pos, preferred_element_type=jnp.float32)
    pushed = lax.dot_general(
        narrow, positions, (((0,), (0,)), ((), ())), preferred_element_type=jnp.float32
    )
    row_term = direct + 2.0 * cost_scale * (row_mass[:, None] * row_f32 - pulled)
    col_term = 2.0 * cost_scale * (col_mass[:, None] * col_f32 - pushed)
    row_part = lax.psum_scatter(
        row_term.astype(jnp.bfloat16), "col", scatter_dimension=0, tiled=True
    ).astype(jnp.float32)
    summed = lax.psum(col_term.astype(jnp.bfloat16), "row").astype(jnp.float32)
    col_part = lax.dynamic_slice_in_dim(summed, lax.axis_index("row") * piece_len, piece_len, 0)
    return (row_part + col_part, grad_log_weights)


def solution(mesh):
    in_specs = (P("row", None), P("row"), P("row", None))
    out_specs = (P(("row", "col"), None), P("row"))
    return jax.shard_map(local, mesh=mesh, in_specs=in_specs, out_specs=out_specs, check_vma=False)
```

profile of v0, /device:TPU:1, one launch (start us, length us, event | category | flops | bytes accessed | tf_op | source)
XLA Modules:
  0.0 1291.2 jit_solution(14466195769258401368)
XLA Ops:
  9.3 27.6 %all_gather.6 = bf16[2048,64]{1,0:T(8,128)(2,1)S(1)} all-gather(bf16[64,64]{1,0:T(8,128)(2,1)S(1)} %constant_dynamic-slice_fusion.1), channel_id=1, replica_groups=mesh['row'=32,'col'=4] {'row'}, dimensions={0}, use_global_device_ids=true | all-gather | bytes 270336 | tf_op jit(solution)/shard_map/all_gather | solution.py:31
  37.3 24.2 %all_gather.7 = bf16[2048,64]{1,0:T(8,128)(2,1)S(1)} all-gather(bf16[64,64]{1,0:T(8,128)(2,1)S(1)} %copy.10), channel_id=1, replica_groups=mesh['row'=32,'col'=4] {'row'}, dimensions={0}, use_global_device_ids=true | all-gather | bytes 270336 | tf_op jit(solution)/shard_map/all_gather | solution.py:32
  62.8 8.5 pmax.70
  78.1 66.9 %pmax.71 = f32[2048]{0:T(1024)S(1)} all-reduce(f32[2048]{0:T(1024)S(1)} %subtract_reduce_fusion.8), channel_id=1, replica_groups=mesh['row'=32,'col'=4] {'row'}, use_global_device_ids=true, to_apply=%region_7.0 | all-reduce | flops 2048 | bytes 16384 | tf_op jit(solution)/shard_map/pmax | solution.py:17
  145.7 63.7 %psum.148 = f32[2048]{0:T(1024)S(1)} all-reduce(f32[2048]{0:T(1024)S(1)} %exponential_reduce_fusion.8), channel_id=1, replica_groups=mesh['row'=32,'col'=4] {'row'}, use_global_device_ids=true, to_apply=%region_9.0 | all-reduce | flops 2048 | bytes 16384 | tf_op jit(solution)/shard_map/psum | solution.py:18
  209.8 7.7 pmax.72
  224.3 67.4 %pmax.73 = f32[2048]{0:T(1024)S(1)} all-reduce(f32[2048]{0:T(1024)S(1)} %subtract_reduce_fusion.6), channel_id=1, replica_groups=mesh['row'=32,'col'=4] {'row'}, use_global_device_ids=true, to_apply=%region_15.0 | all-reduce | flops 2048 | bytes 16384 | tf_op jit(solution)/shard_map/pmax | solution.py:17
  292.5 63.7 %psum.150 = f32[2048]{0:T(1024)S(1)} all-reduce(f32[2048]{0:T(1024)S(1)} %exponential_reduce_fusion.6), channel_id=1, replica_groups=mesh['row'=32,'col'=4] {'row'}, use_global_device_ids=true, to_apply=%region_17.0 | all-reduce | flops 2048 | bytes 16384 | tf_op jit(solution)/shard_map/psum | solution.py:18
  356.5 7.7 pmax.74
  371.1 67.4 %pmax.75 = f32[2048]{0:T(1024)S(1)} all-reduce(f32[2048]{0:T(1024)S(1)} %subtract_reduce_fusion.4), channel_id=1, replica_groups=mesh['row'=32,'col'=4] {'row'}, use_global_device_ids=true, to_apply=%region_23.0 | all-reduce | flops 2048 | bytes 16384 | tf_op jit(solution)/shard_map/pmax | solution.py:17
  439.2 63.7 %psum.152 = f32[2048]{0:T(1024)S(1)} all-reduce(f32[2048]{0:T(1024)S(1)} %exponential_reduce_fusion.4), channel_id=1, replica_groups=mesh['row'=32,'col'=4] {'row'}, use_global_device_ids=true, to_apply=%region_25.0 | all-reduce | flops 2048 | bytes 16384 | tf_op jit(solution)/shard_map/psum | solution.py:18
  503.3 7.7 pmax.76
  518.0 67.4 %pmax.77 = f32[2048]{0:T(1024)S(1)} all-reduce(f32[2048]{0:T(1024)S(1)} %subtract_reduce_fusion.2), channel_id=1, replica_groups=mesh['row'=32,'col'=4] {'row'}, use_global_device_ids=true, to_apply=%region_31.0 | all-reduce | flops 2048 | bytes 16384 | tf_op jit(solution)/shard_map/pmax | solution.py:17
  586.2 63.7 %psum.154 = f32[2048]{0:T(1024)S(1)} all-reduce(f32[2048]{0:T(1024)S(1)} %exponential_reduce_fusion.2), channel_id=1, replica_groups=mesh['row'=32,'col'=4] {'row'}, use_global_device_ids=true, to_apply=%region_33.0 | all-reduce | flops 2048 | bytes 16384 | tf_op jit(solution)/shard_map/psum | solution.py:18
  664.8 67.4 %pmax.79 = f32[2048]{0:T(1024)S(1)} all-reduce(f32[2048]{0:T(1024)S(1)} %subtract_reduce_fusion), channel_id=1, replica_groups=mesh['row'=32,'col'=4] {'row'}, use_global_device_ids=true, to_apply=%region_39.0 | all-reduce | flops 2048 | bytes 16384 | tf_op jit(solution)/shard_map/pmax | solution.py:17
  732.9 63.7 %psum.156 = f32[2048]{0:T(1024)S(1)} all-reduce(f32[2048]{0:T(1024)S(1)} %exponential_reduce_fusion), channel_id=1, replica_groups=mesh['row'=32,'col'=4] {'row'}, use_global_device_ids=true, to_apply=%region_41.0 | all-reduce | flops 2048 | bytes 16384 | tf_op jit(solution)/shard_map/psum | solution.py:18
  799.6 63.7 %psum.157 = f32[2048]{0:T(1024)S(1)} all-reduce(f32[2048]{0:T(1024)S(1)} %get-tuple-element.4), channel_id=1, replica_groups=mesh['row'=32,'col'=4] {'row'}, use_global_device_ids=true, to_apply=%region_43.0 | all-reduce | flops 2048 | bytes 16384 | tf_op jit(solution)/shard_map/psum | solution.py:66
  872.6 65.7 %psum.159 = f32[2048]{0:T(1024)S(1)} all-reduce(f32[2048]{0:T(1024)S(1)} %fusion.12), channel_id=1, replica_groups=mesh['row'=32,'col'=4] {'row'}, use_global_device_ids=true, to_apply=%region_48.0 | all-reduce | flops 2048 | bytes 16384 | tf_op jit(solution)/shard_map/psum | solution.py:84
  945.9 65.4 %psum.161 = f32[2048]{0:T(1024)S(1)} all-reduce(f32[2048]{0:T(1024)S(1)} %fusion.13), channel_id=1, replica_groups=mesh['row'=32,'col'=4] {'row'}, use_global_device_ids=true, to_apply=%region_52.0 | all-reduce | flops 2048 | bytes 16384 | tf_op jit(solution)/shard_map/psum | solution.py:84
  1020.6 65.7 %psum.163 = f32[2048]{0:T(1024)S(1)} all-reduce(f32[2048]{0:T(1024)S(1)} %fusion.14), channel_id=1, replica_groups=mesh['row'=32,'col'=4] {'row'}, use_global_device_ids=true, to_apply=%region_56.0 | all-reduce | flops 2048 | bytes 16384 | tf_op jit(solution)/shard_map/psum | solution.py:84
  1093.9 65.4 %psum.165 = f32[2048]{0:T(1024)S(1)} all-reduce(f32[2048]{0:T(1024)S(1)} %fusion.15), channel_id=1, replica_groups=mesh['row'=32,'col'=4] {'row'}, use_global_device_ids=true, to_apply=%region_60.0 | all-reduce | flops 2048 | bytes 16384 | tf_op jit(solution)/shard_map/psum | solution.py:84
  1167.8 8.2 fusion.25
  1181.3 11.4 reduce-scatter.2.cloned.1.call-done
  1192.7 89.7 %all-reduce.2.cloned.1.call-done = bf16[2048,64]{1,0:T(8,128)(2,1)} async-done(((bf16[2048,64]{1,0:T(8,128)(2,1)}), bf16[2048,64]{1,0:T(8,128)(2,1)}) %all-reduce.2.cloned.1.call-update) | async-done | bytes 262160 | tf_op jit(solution)/shard_map/psum | solution.py:98
  (83 shorter events, 101.3 us)
Async XLA Ops:
  8.0 1.1 copy-start
  8.0 1184.7 %reduce-scatter.2.cloned.1.call-start = ((), (), s32[]{:S(2)}) async-start(), calls=%async_computation.1 | async-start | bytes 81920 | tf_op jit(solution)/shard_map/reduce_scatter | solution.py:95
  61.5 16.2 %copy-start.3 = (f32[256]{0:T(256)S(1)}, f32[256]{0:T(256)}, u32[]{:S(2)}) copy-start(f32[256]{0:T(256)} %param.4) | copy-start | bytes 3076
  732.9 64.6 %copy-start.2 = (bf16[256,64]{0,1:T(8,128)(2,1)S(1)}, bf16[256,64]{0,1:T(8,128)(2,1)}, u32[]{:S(2)}) copy-start(bf16[256,64]{0,1:T(8,128)(2,1)} %param.3) | copy-start | bytes 98308
  1176.0 1.0 copy-start.1
  1178.1 104.3 %all-reduce.2.cloned.1.call-start = ((), (), s32[]{:S(2)}) async-start(), calls=%async_computation.2 | async-start | bytes 1048576 | tf_op jit(solution)/shard_map/psum | solution.py:98
Sparse Core Ops, SparseCore 0:
  1178.3 14.3 reduce-scatter.1
Sparse Core Ops, SparseCore 1:
  1181.8 100.5 all-reduce.1
where the time goes:
time: 1290 us
  blocking collectives  1140 us (88%)
  waiting for transfers between devices  101 us (8%)
  other arithmetic  26.4 us (2%)
  between operations  15.9 us (1%)
    pmax x5, blocking collectives, column_lse(): highest = lax.pmax(jnp.max(logits, axis=0), 'row')  337 us
    psum x5, blocking collectives, column_lse(): lax.psum(jnp.sum(jnp.exp(logits - highest[None, :]), axis=0), 'row')  318 us
    psum x4, blocking collectives, local(): col_grad = -lax.psum(jnp.sum(back_tile * row_grad[:, None], axis=0), 'row')  262 us
    psum x1, waiting for transfers between devices, local(): summed = lax.psum(col_term.astype(jnp.bfloat16), 'row').astype(jnp.float32)  89.7 us
    psum x1, blocking collectives, local(): col_grad = lax.psum(jnp.sum(weighted, axis=0), 'row')  63.7 us
    pmax x5, blocking collectives, row_lse(): highest = lax.pmax(jnp.max(logits, axis=1), 'col')  39.4 us
    psum x5, blocking collectives, local(): lax.psum(surplus - jnp.sum(column_soft * col_grad[None, :], axis=1), 'col')  35.2 us
    psum x5, blocking collectives, row_lse(): lax.psum(jnp.sum(jnp.exp(logits - highest[:, None]), axis=1), 'col')  30.3 us
  transfers between devices with their start and end apart: 2, of which 2 were waited for; matrix products, arithmetic and copies ran while one was open for 0% of the time, Pallas kernels for 0%

commit v1 on v0

--- a/solution.py
+++ b/solution.py
@@ -81,7 +81,9 @@
         )
         grad_log_weights = grad_log_weights + row_grad
         if section > 0:
-            col_grad = -lax.psum(jnp.sum(back_tile * row_grad[:, None], axis=0), "row")
+            col_grad = -jnp.sum(
+                lax.all_gather(jnp.sum(back_tile * row_grad[:, None], axis=0), "row"), axis=0
+            )
     row_mass = jnp.sum(gradient_tile, axis=1)
     col_mass = jnp.sum(gradient_tile, axis=0)
     narrow = gradient_tile.astype(jnp.bfloat16)

time: 1290 us -> 1130 us (0.88)
  blocking collectives: 1140 us -> 977 us
    psum x4 -> x0, blocking collectives: 262 us -> none  [local(): col_grad = -lax.psum(jnp.sum(back_tile * row_grad[:, None], axis=0), 'row')]
    all_gather x0 -> x4, blocking collectives: none -> 102 us  [local(): lax.all_gather(jnp.sum(back_tile * row_grad[:, None], axis=0), 'row')]
where the time goes in v1:
time: 1130 us
  blocking collectives  977 us (86%)
  waiting for transfers between devices  103 us (9%)
  other arithmetic  26.5 us (2%)
  between operations  15.9 us (1%)
    pmax x5, blocking collectives, column_lse(): highest = lax.pmax(jnp.max(logits, axis=0), 'row')  337 us
    psum x5, blocking collectives, column_lse(): lax.psum(jnp.sum(jnp.exp(logits - highest[None, :]), axis=0), 'row')  318 us
    all_gather x4, blocking collectives, local(): lax.all_gather(jnp.sum(back_tile * row_grad[:, None], axis=0), 'row')  102 us
    psum x1, waiting for transfers between devices, local(): summed = lax.psum(col_term.astype(jnp.bfloat16), 'row').astype(jnp.float32)  89.6 us
    psum x1, blocking collectives, local(): col_grad = lax.psum(jnp.sum(weighted, axis=0), 'row')  63.7 us
    pmax x5, blocking collectives, row_lse(): highest = lax.pmax(jnp.max(logits, axis=1), 'col')  39.4 us
    psum x5, blocking collectives, local(): lax.psum(surplus - jnp.sum(column_soft * col_grad[None, :], axis=1), 'col')  35.4 us
    psum x5, blocking collectives, row_lse(): lax.psum(jnp.sum(jnp.exp(logits - highest[:, None]), axis=1), 'col')  30.3 us
  transfers between devices with their start and end apart: 2, of which 2 were waited for; matrix products, arithmetic and copies ran while one was open for 0% of the time, Pallas kernels for 0%

profile of v1, /device:TPU:1, one launch (start us, length us, event | category | flops | bytes accessed | tf_op | source)
XLA Modules:
  0.0 1132.7 jit_solution(15599880139264808410)
XLA Ops:
  9.3 27.6 %all_gather.30 = bf16[2048,64]{1,0:T(8,128)(2,1)S(1)} all-gather(bf16[64,64]{1,0:T(8,128)(2,1)S(1)} %constant_dynamic-slice_fusion.1), channel_id=1, replica_groups=mesh['row'=32,'col'=4] {'row'}, dimensions={0}, use_global_device_ids=true | all-gather | bytes 270336 | tf_op jit(solution)/shard_map/all_gather | solution.py:31
  37.3 24.2 %all_gather.31 = bf16[2048,64]{1,0:T(8,128)(2,1)S(1)} all-gather(bf16[64,64]{1,0:T(8,128)(2,1)S(1)} %copy.13), channel_id=1, replica_groups=mesh['row'=32,'col'=4] {'row'}, dimensions={0}, use_global_device_ids=true | all-gather | bytes 270336 | tf_op jit(solution)/shard_map/all_gather | solution.py:32
  62.8 8.5 pmax.70
  78.1 66.9 %pmax.71 = f32[2048]{0:T(1024)S(1)} all-reduce(f32[2048]{0:T(1024)S(1)} %subtract_reduce_fusion.8), channel_id=1, replica_groups=mesh['row'=32,'col'=4] {'row'}, use_global_device_ids=true, to_apply=%region_7.0 | all-reduce | flops 2048 | bytes 16384 | tf_op jit(solution)/shard_map/pmax | solution.py:17
  145.7 63.7 %psum.120 = f32[2048]{0:T(1024)S(1)} all-reduce(f32[2048]{0:T(1024)S(1)} %exponential_reduce_fusion.8), channel_id=1, replica_groups=mesh['row'=32,'col'=4] {'row'}, use_global_device_ids=true, to_apply=%region_9.0 | all-reduce | flops 2048 | bytes 16384 | tf_op jit(solution)/shard_map/psum | solution.py:18
  224.3 67.4 %pmax.73 = f32[2048]{0:T(1024)S(1)} all-reduce(f32[2048]{0:T(1024)S(1)} %subtract_reduce_fusion.6), channel_id=1, replica_groups=mesh['row'=32,'col'=4] {'row'}, use_global_device_ids=true, to_apply=%region_15.0 | all-reduce | flops 2048 | bytes 16384 | tf_op jit(solution)/shard_map/pmax | solution.py:17
  292.5 63.7 %psum.122 = f32[2048]{0:T(1024)S(1)} all-reduce(f32[2048]{0:T(1024)S(1)} %exponential_reduce_fusion.6), channel_id=1, replica_groups=mesh['row'=32,'col'=4] {'row'}, use_global_device_ids=true, to_apply=%region_17.0 | all-reduce | flops 2048 | bytes 16384 | tf_op jit(solution)/shard_map/psum | solution.py:18
  371.1 67.4 %pmax.75 = f32[2048]{0:T(1024)S(1)} all-reduce(f32[2048]{0:T(1024)S(1)} %subtract_reduce_fusion.4), channel_id=1, replica_groups=mesh['row'=32,'col'=4] {'row'}, use_global_device_ids=true, to_apply=%region_23.0 | all-reduce | flops 2048 | bytes 16384 | tf_op jit(solution)/shard_map/pmax | solution.py:17
  439.2 63.7 %psum.124 = f32[2048]{0:T(1024)S(1)} all-reduce(f32[2048]{0:T(1024)S(1)} %exponential_reduce_fusion.4), channel_id=1, replica_groups=mesh['row'=32,'col'=4] {'row'}, use_global_device_ids=true, to_apply=%region_25.0 | all-reduce | flops 2048 | bytes 16384 | tf_op jit(solution)/shard_map/psum | solution.py:18
  518.0 67.4 %pmax.77 = f32[2048]{0:T(1024)S(1)} all-reduce(f32[2048]{0:T(1024)S(1)} %subtract_reduce_fusion.2), channel_id=1, replica_groups=mesh['row'=32,'col'=4] {'row'}, use_global_device_ids=true, to_apply=%region_31.0 | all-reduce | flops 2048 | bytes 16384 | tf_op jit(solution)/shard_map/pmax | solution.py:17
  586.2 63.7 %psum.126 = f32[2048]{0:T(1024)S(1)} all-reduce(f32[2048]{0:T(1024)S(1)} %exponential_reduce_fusion.2), channel_id=1, replica_groups=mesh['row'=32,'col'=4] {'row'}, use_global_device_ids=true, to_apply=%region_33.0 | all-reduce | flops 2048 | bytes 16384 | tf_op jit(solution)/shard_map/psum | solution.py:18
  664.8 67.4 %pmax.79 = f32[2048]{0:T(1024)S(1)} all-reduce(f32[2048]{0:T(1024)S(1)} %subtract_reduce_fusion), channel_id=1, replica_groups=mesh['row'=32,'col'=4] {'row'}, use_global_device_ids=true, to_apply=%region_39.0 | all-reduce | flops 2048 | bytes 16384 | tf_op jit(solution)/shard_map/pmax | solution.py:17
  732.9 63.7 %psum.128 = f32[2048]{0:T(1024)S(1)} all-reduce(f32[2048]{0:T(1024)S(1)} %exponential_reduce_fusion), channel_id=1, replica_groups=mesh['row'=32,'col'=4] {'row'}, use_global_device_ids=true, to_apply=%region_41.0 | all-reduce | flops 2048 | bytes 16384 | tf_op jit(solution)/shard_map/psum | solution.py:18
  799.5 63.7 %psum.129 = f32[2048]{0:T(1024)S(1)} all-reduce(f32[2048]{0:T(1024)S(1)} %get-tuple-element.4), channel_id=1, replica_groups=mesh['row'=32,'col'=4] {'row'}, use_global_device_ids=true, to_apply=%region_43.0 | all-reduce | flops 2048 | bytes 16384 | tf_op jit(solution)/shard_map/psum | solution.py:66
  864.0 7.7 psum.130
  872.5 24.5 %all-gather = f32[65536]{0:T(1024)S(1)} all-gather(f32[2048]{0:T(1024)S(1)} %fusion.12), channel_id=2, replica_groups=mesh['row'=32,'col'=4] {'row'}, dimensions={0}, use_global_device_ids=true | all-gather | bytes 270336 | tf_op jit(solution)/shard_map/all_gather | solution.py:85
  904.7 26.7 %all-gather.1 = f32[65536]{0:T(1024)S(1)} all-gather(f32[2048]{0:T(1024)S(1)} %fusion.13), channel_id=3, replica_groups=mesh['row'=32,'col'=4] {'row'}, dimensions={0}, use_global_device_ids=true | all-gather | bytes 270336 | tf_op jit(solution)/shard_map/all_gather | solution.py:85
  932.2 7.9 psum.132
  940.9 24.0 %all-gather.2 = f32[65536]{0:T(1024)S(1)} all-gather(f32[2048]{0:T(1024)S(1)} %fusion.14), channel_id=4, replica_groups=mesh['row'=32,'col'=4] {'row'}, dimensions={0}, use_global_device_ids=true | all-gather | bytes 270336 | tf_op jit(solution)/shard_map/all_gather | solution.py:85
  972.5 26.7 %all-gather.3 = f32[65536]{0:T(1024)S(1)} all-gather(f32[2048]{0:T(1024)S(1)} %fusion.15), channel_id=5, replica_groups=mesh['row'=32,'col'=4] {'row'}, dimensions={0}, use_global_device_ids=true | all-gather | bytes 270336 | tf_op jit(solution)/shard_map/all_gather | solution.py:85
  1000.0 7.7 psum.134
  1007.8 8.2 fusion.25
  1021.2 13.0 %reduce-scatter.2.cloned.1.call-done = bf16[64,64]{1,0:T(8,128)(2,1)} async-done(((bf16[256,64]{1,0:T(8,128)(2,1)}), bf16[64,64]{1,0:T(8,128)(2,1)}) %reduce-scatter.2.cloned.1.call-update) | async-done | bytes 8208 | tf_op jit(solution)/shard_map/reduce_scatter | solution.py:97
  1034.2 89.6 %all-reduce.2.cloned.1.call-done = bf16[2048,64]{1,0:T(8,128)(2,1)} async-done(((bf16[2048,64]{1,0:T(8,128)(2,1)}), bf16[2048,64]{1,0:T(8,128)(2,1)}) %all-reduce.2.cloned.1.call-update) | async-done | bytes 262160 | tf_op jit(solution)/shard_map/psum | solution.py:100
  (91 shorter events, 101.6 us)
Async XLA Ops:
  8.0 1.1 copy-start
  8.0 1026.2 %reduce-scatter.2.cloned.1.call-start = ((), (), s32[]{:S(2)}) async-start(), calls=%async_computation.1 | async-start | bytes 81920 | tf_op jit(solution)/shard_map/reduce_scatter | solution.py:97
  61.5 16.2 %copy-start.3 = (f32[256]{0:T(256)S(1)}, f32[256]{0:T(256)}, u32[]{:S(2)}) copy-start(f32[256]{0:T(256)} %param.4) | copy-start | bytes 3076
  732.9 64.6 %copy-start.2 = (bf16[256,64]{0,1:T(8,128)(2,1)S(1)}, bf16[256,64]{0,1:T(8,128)(2,1)}, u32[]{:S(2)}) copy-start(bf16[256,64]{0,1:T(8,128)(2,1)} %param.3) | copy-start | bytes 98308
  1016.0 1.0 copy-start.1
  1018.1 105.8 %all-reduce.2.cloned.1.call-start = ((), (), s32[]{:S(2)}) async-start(), calls=%async_computation.2 | async-start | bytes 1048576 | tf_op jit(solution)/shard_map/psum | solution.py:100
Sparse Core Ops, SparseCore 0:
  1018.2 15.9 reduce-scatter.1
Sparse Core Ops, SparseCore 1:
  1021.8 102.0 all-reduce.1
